TPU v7x, 512 devices: a whole 4x8x8 slice. The times are simulated.
512 devices in a mesh: dp: 8 (over y), row: 4 (over z_lo), col: 16 (over x, z_hi, core).
Axes of the slice: x: 4, y: 8, z: 8 (z_hi: 2, z_lo: 4; z = z_hi * 4 + z_lo), core: 2. Of those that a mesh axis runs over, the one named last changes fastest.
Arguments:
- tokens: bfloat16 [2048, 4096], P(('dp', 'col'), 'row'), may hold values from -6 to 6
- gate_weight: bfloat16 [4096, 14336], P('row', 'col'), may hold values from -0.125 to 0.125
- up_weight: bfloat16 [4096, 14336], P('row', 'col'), may hold values from -0.125 to 0.125
- gate_mask: int32 [32, 112], P('row', 'col'), may hold values 0 or 1
- up_mask: int32 [32, 112], P('row', 'col'), may hold values 0 or 1
- slope: bfloat16 [2048, 14336], P(('dp', 'row'), 'col'), may hold values from -6 to 6
Outputs:
- hidden: bfloat16 [2048, 14336], P(('dp', 'row'), 'col')
- input_grad: bfloat16 [2048, 4096], P(('dp', 'col'), 'row')
- gate_grad: bfloat16 [32, 128, 14336], P('row', 'dp', 'col')
- up_grad: bfloat16 [32, 128, 14336], P('row', 'dp', 'col')
Inputs may be any that keep to these rules, and one draw needn't show every extreme that they name: `gate_mask`: 1 marks a live 128 x 128 block of the projection, 0 a pruned one. `up_mask`: 1 marks a live 128 x 128 block of the projection, 0 a pruned one.
All inputs are finite; a program needn't handle non-finite values.
Results may differ from a plain program's by a relative error of at most 0.0058.
Values may be sent and summed in bfloat16 or wider, within the bound.
No kernel may reach another device: no remote copies, remote signals or barrier semaphores. Data moves between devices by JAX's collectives and lax.ppermute only.
A program may use at most 64 MiB of HBM per device.

v0:
```python
import jax
import jax.numpy as jnp
from jax import lax
from jax.experimental import pallas as pl
from jax.experimental.pallas import tpu as pltpu
from jax.sharding import PartitionSpec as P

BF = jnp.bfloat16
F32 = jnp.float32
MIB = 1024 * 1024
ROWS = 256


def in_smem():
    return pl.BlockSpec(memory_space=pltpu.SMEM)


def in_vmem():
    return pl.BlockSpec(memory_space=pltpu.VMEM)


def prune(live, gate_w, up_w, gate_mask, up_mask, block, first):
    for b in range(live.shape[0] // block):
        part = pl.ds(b * block, block)
        for j in range(gate_mask.shape[1]):
            one = pl.ds(j * block, block)
            for k, (w, m) in enumerate(((gate_w, gate_mask), (up_w, up_mask))):
                alive = m[first + b, j].astype(F32).astype(BF)
                live[part, pl.ds((2 * j + k) * block, block)] = w[part, one] * alive


def forward(tokens, gate_weight, up_weight, gate_mask, up_mask):
    depth, width = gate_weight.shape
    block = depth // gate_mask.shape[0]
    toks = tokens.shape[0]
    steps = depth // ROWS

    def kernel(gm, um, t, gw, uw, out, live, total):
        step = pl.program_id(0)
        prune(live, gw, uw, gm, um, block, step * (ROWS // block))
        term = jnp.dot(t[...], live[...], preferred_element_type=F32)

        @pl.when(step == 0)
        def _():
            total[...] = term

        @pl.when((step > 0) & (step < steps - 1))
        def _():
            total[...] += term

        @pl.when(step == steps - 1)
        def _():
            out[...] = (total[...] + term).astype(BF)

    return pl.pallas_call(
        kernel,
        grid=(steps,),
        in_specs=[
            in_smem(),
            in_smem(),
            pl.BlockSpec((toks, ROWS), lambda k: (0, k)),
            pl.BlockSpec((ROWS, width), lambda k: (k, 0)),
            pl.BlockSpec((ROWS, width), lambda k: (k, 0)),
        ],
        out_specs=pl.BlockSpec((toks, 2 * width), lambda k: (0, 0)),
        out_shape=jax.ShapeDtypeStruct((toks, 2 * width), BF),
        scratch_shapes=[pltpu.VMEM((ROWS, 2 * width), BF), pltpu.VMEM((toks, 2 * width), F32)],
        cost_estimate=pl.CostEstimate(
            flops=4 * toks * depth * width,
            bytes_accessed=4 * depth * width + 6 * toks * depth,
            transcendentals=0,
        ),
        compiler_params=pltpu.CompilerParams(vmem_limit_bytes=60 * MIB),
        name="forward",
    )(gate_mask, up_mask, tokens, gate_weight, up_weight)


def activate(received, slope, block, sources):
    here, width = slope.shape
    count = width // block

    def kernel(r, s, hidden, slopes):
        for j in range(count):
            both = pl.ds(2 * j * block, 2 * block)
            total = r[pl.ds(0, here), both].astype(F32)
            for k in range(1, sources):
                total = total + r[pl.ds(k * here, here), both].astype(F32)
            gate, up = total[:, :block], total[:, block:]
            sigma = jax.nn.sigmoid(gate)
            act = gate * sigma
            one = pl.ds(j * block, block)
            hidden[:, one] = (act * up).astype(BF)
            wide = s[:, one].astype(F32)
            gate_slope = (wide * up * sigma * (1.0 + gate * (1.0 - sigma))).astype(BF)
            slopes[:, both] = jnp.concatenate([gate_slope, (wide * act).astype(BF)], axis=1)

    return pl.pallas_call(
        kernel,
        in_specs=[in_vmem(), in_vmem()],
        out_specs=[in_vmem(), in_vmem()],
        out_shape=[
            jax.ShapeDtypeStruct((here, width), BF),
            jax.ShapeDtypeStruct((here, 2 * width), BF),
        ],
        cost_estimate=pl.CostEstimate(
            flops=30 * here * width,
            bytes_accessed=here * width * 24,
            transcendentals=here * width,
        ),
        compiler_params=pltpu.CompilerParams(vmem_limit_bytes=12 * MIB),
        name="activate",
    )(received, slope)


def turn(tokens, here, way, block, replicas, reach):
    toks, depth = tokens.shape
    share = block // replicas
    blocks_down = depth // block

    def kernel(place, t, out, turned):
        turned[...] = t[...].T
        for k in range(reach):
            owner = lax.rem(place[0] + place[1] * k + replicas, replicas)
            for b in range(blocks_down):
                rows = pl.ds(pl.multiple_of(b * block + owner * share, share), share)
                out[k, pl.ds(b * share, share), :] = turned[rows, :]

    return pl.pallas_call(
        kernel,
        in_specs=[in_smem(), in_vmem()],
        out_specs=in_vmem(),
        out_shape=jax.ShapeDtypeStruct((reach, blocks_down * share, toks), BF),
        scratch_shapes=[pltpu.VMEM((depth, toks), BF)],
        cost_estimate=pl.CostEstimate(
            flops=0, bytes_accessed=4 * toks * depth, transcendentals=0
        ),
        compiler_params=pltpu.CompilerParams(vmem_limit_bytes=8 * MIB),
        name="turn",
    )(jnp.stack([here, way]), tokens)


def parts_of(turned, slopes, wanted):
    each, toks = turned.shape[1:]
    width = slopes.shape[1]

    def kernel(t, s, *outs):
        for k, out in zip(wanted, outs):
            out[...] = jnp.dot(t[k], s[...], preferred_element_type=F32).astype(BF)

    return pl.pallas_call(
        kernel,
        in_specs=[in_vmem(), in_vmem()],
        out_specs=[in_vmem()] * len(wanted),
        out_shape=[jax.ShapeDtypeStruct((each, width), BF) for _ in wanted],
        cost_estimate=pl.CostEstimate(
            flops=2 * toks * each * width * len(wanted),
            bytes_accessed=2 * each * width * len(wanted),
            transcendentals=0,
        ),
        compiler_params=pltpu.CompilerParams(vmem_limit_bytes=10 * MIB),
    )(turned, slopes)


def plus(arrived, part):
    def kernel(a, p, out):
        out[...] = (a[...].astype(F32) + p[...].astype(F32)).astype(BF)

    size = part.shape[0] * part.shape[1]
    return pl.pallas_call(
        kernel,
        in_specs=[in_vmem(), in_vmem()],
        out_specs=in_vmem(),
        out_shape=jax.ShapeDtypeStruct(part.shape, BF),
        cost_estimate=pl.CostEstimate(flops=size, bytes_accessed=6 * size, transcendentals=0),
        compiler_params=pltpu.CompilerParams(vmem_limit_bytes=6 * MIB),
        name="plus",
    )(arrived, part)


def backward(slopes, gate_weight, up_weight, gate_mask, up_mask):
    depth, width = gate_weight.shape
    block = depth // gate_mask.shape[0]
    toks = slopes.shape[0]

    def kernel(gm, um, s, gw, uw, out, live):
        prune(live, gw, uw, gm, um, block, pl.program_id(0) * (ROWS // block))
        out[...] = lax.dot_general(
            s[...], live[...], (((1,), (1,)), ((), ())), preferred_element_type=F32
        )

    return pl.pallas_call(
        kernel,
        grid=(depth // ROWS,),
        in_specs=[
            in_smem(),
            in_smem(),
            pl.BlockSpec((toks, 2 * width), lambda k: (0, 0)),
            pl.BlockSpec((ROWS, width), lambda k: (k, 0)),
            pl.BlockSpec((ROWS, width), lambda k: (k, 0)),
        ],
        out_specs=pl.BlockSpec((toks, ROWS), lambda k: (0, k)),
        out_shape=jax.ShapeDtypeStruct((toks, depth), F32),
        scratch_shapes=[pltpu.VMEM((ROWS, 2 * width), BF)],
        cost_estimate=pl.CostEstimate(
            flops=4 * toks * depth * width,
            bytes_accessed=4 * depth * width + 6 * toks * depth,
            transcendentals=0,
        ),
        compiler_params=pltpu.CompilerParams(vmem_limit_bytes=20 * MIB),
        name="backward",
    )(gate_mask, up_mask, slopes, gate_weight, up_weight)


def reduce_parts(turned, slopes, weights):
    replicas = lax.axis_size("dp")
    cols = lax.axis_size("col")
    far = replicas // 2
    ring = [
        (p * cols + c, (p + 1 - 2 * (c % 2)) % replicas * cols + c)
        for p in range(replicas)
        for c in range(cols)
    ]
    swap = [(c, c ^ 1) for c in range(cols)]
    own = parts_of(turned, slopes, [far])[0]
    other_slopes = lax.ppermute(slopes, "col", swap)
    near = list(range(far - 1, 0, -1))
    own_parts = parts_of(turned, slopes, near + [0])
    share = backward(slopes, *weights)
    other_parts = parts_of(turned, other_slopes, near)
    other = other_parts[0]
    for hop in range(far):
        own = lax.ppermute(own, ("dp", "col"), ring)
        if hop < far - 1:
            own = plus(own, own_parts[hop])
            other = lax.ppermute(other, ("dp", "col"), ring)
            if hop < far - 2:
                other = plus(other, other_parts[hop + 1])
    other = lax.ppermute(other, "col", swap)
    return (own, other, own_parts[far - 1]), share


def finish(sums, gate_mask, up_mask, block):
    each, _ = sums[0].shape
    blocks_down, total = gate_mask.shape
    share = each // blocks_down

    def kernel(gm, um, *refs):
        gate_out, up_out = refs[-2], refs[-1]
        for c in range(total):
            both = pl.ds(2 * c * block, 2 * block)
            columns = pl.ds(c * block, block)
            whole = refs[0][:, both].astype(F32)
            for r in refs[1:-2]:
                whole = whole + r[:, both].astype(F32)
            for b in range(blocks_down):
                part = whole[b * share : (b + 1) * share]
                gate_out[b, :, columns] = (part[:, :block] * gm[b, c].astype(F32)).astype(BF)
                up_out[b, :, columns] = (part[:, block:] * um[b, c].astype(F32)).astype(BF)

    shape = jax.ShapeDtypeStruct((blocks_down, share, total * block), BF)
    return pl.pallas_call(
        kernel,
        in_specs=[in_smem(), in_smem()] + [in_vmem()] * len(sums),
        out_specs=[in_vmem(), in_vmem()],
        out_shape=[shape, shape],
        compiler_params=pltpu.CompilerParams(vmem_limit_bytes=8 * MIB),
        name="finish",
    )(gate_mask, up_mask, *sums)


def gather_tokens(tokens):
    cols = lax.axis_size("col")
    near = 4
    same_x = [list(range(i, i + near)) for i in range(0, cols, near)]
    along_x = [list(range(i, cols, near)) for i in range(near)]
    tokens = lax.all_gather(tokens, "col", axis=0, tiled=True, axis_index_groups=same_x)
    return lax.all_gather(tokens, "col", axis=0, tiled=True, axis_index_groups=along_x)


def body(tokens, gate_weight, up_weight, gate_mask, up_mask, slope):
    block = gate_weight.shape[0] // gate_mask.shape[0]
    rows = lax.axis_size("row")
    replicas = lax.axis_size("dp")
    cols = lax.axis_size("col")
    weights = (gate_weight, up_weight, gate_mask, up_mask)
    here = lax.axis_index("dp").astype(jnp.int32)
    way = 1 - 2 * (lax.axis_index("col").astype(jnp.int32) % 2)
    return layer(tokens, weights, slope, block, rows, replicas, cols, here, way)


def layer(tokens, weights, slope, block, rows, replicas, cols, here, way):
    gathered = gather_tokens(tokens)
    partial = forward(gathered, *weights)
    received = lax.all_to_all(partial, "row", 0, 0, tiled=True)
    turned = turn(gathered, here, way, block, replicas, replicas // 2 + 1)
    hidden, slopes = activate(received, slope, block, rows)
    slopes = lax.all_gather(slopes, "row", axis=0, tiled=True)
    sums, share = reduce_parts(turned, slopes, weights)
    pieces = lax.all_to_all(share, "col", 0, 0, tiled=True)
    input_grad = jnp.sum(pieces.reshape((cols, -1) + pieces.shape[1:]), axis=0).astype(BF)
    gate_grad, up_grad = finish(sums, weights[2], weights[3], block)
    return hidden, input_grad, gate_grad, up_grad


def solution(mesh):
    return jax.shard_map(
        body,
        mesh=mesh,
        in_specs=(
            P(("dp", "col"), "row"),
            P("row", "col"),
            P("row", "col"),
            P("row", "col"),
            P("row", "col"),
            P(("dp", "row"), "col"),
        ),
        out_specs=(
            P(("dp", "row"), "col"),
            P(("dp", "col"), "row"),
            P("row", "dp", "col"),
            P("row", "dp", "col"),
        ),
        check_vma=False,
    )
```

profile of v0, /device:TPU:6, one launch (start us, length us, event | category | flops | bytes accessed | tf_op | source)
XLA Modules:
  0.0 144.7 jit_solution(5309303162405095240)
XLA Ops:
  0.6 12.8 %all_gather.9 = bf16[64,1024]{1,0:T(8,128)(2,1)S(1)} all-gather(bf16[16,1024]{1,0:T(8,128)(2,1)} %param.6), channel_id=1, replica_groups={{0,1,2,3},{4,5,6,7},{8,9,10,11},{12,13,14,15},{16,17,18,19},{20,21,22,2..., dimensions={0}, use_global_device_ids=true | all-gather | bytes 163840 | tf_op jit(solution)/shard_map/all_gather | solution.py:276
  13.5 13.6 %all_gather.10.t = bf16[256,1024]{1,0:T(8,128)(2,1)} all-gather(bf16[64,1024]{1,0:T(8,128)(2,1)S(1)} %all_gather.9), channel_id=1, replica_groups={{0,4,8,12},{1,5,9,13},{2,6,10,14},{3,7,11,15},{16,20,24,28},{17,21,25,2..., dimensions={0}, use_global_device_ids=true | all-gather | bytes 655360 | tf_op jit(solution)/shard_map/all_gather | solution.py:277
  27.0 5.4 %forward.1 = bf16[256,1792]{1,0:T(8,128)(2,1)} custom-call(s32[8,7]{1,0:T(8,128)} %gm.5, s32[8,7]{1,0:T(8,128)} %um.5, bf16[256,1024]{1,0:T(8,128)(2,1)} %all_gather.10.t, bf16[1024,896]{1,0:T(8,128)(2,1)} %gw.3, bf16[1024,896]{1,0:T(8,128)(2,1)} %uw.3), custom_call_target="tpu_custom_call" | custom-call | flops 939524096 | bytes 5242880 | tf_op jit(solution)/shard_map/forward/pallas_call | solution.py:55
  32.5 0.0 copy-start.4
  32.5 0.0 copy-start
  32.5 0.0 copy-start.5
  32.5 0.0 copy-start.6
  32.5 25.5 %all_to_all.20 = bf16[4,64,1792]{2,1,0:T(8,128)(2,1)S(1)} all-to-all(bf16[4,64,1792]{2,1,0:T(8,128)(2,1)} %bitcast.7), channel_id=1, replica_groups=mesh['dp'=8,'row'=4,'col'=16] {'row'}, dimensions={0} | all-to-all | bytes 1835008 | tf_op jit(solution)/shard_map/all_to_all | solution.py:294
  57.9 0.0 copy-done.4
  57.9 0.8 activate.1
  58.7 19.1 %all_gather.11.s = bf16[256,1792]{1,0:T(8,128)(2,1)S(1)} all-gather(bf16[64,1792]{1,0:T(8,128)(2,1)S(1)} %get-tuple-element.16), channel_id=1, replica_groups=mesh['dp'=8,'row'=4,'col'=16] {'row'}, dimensions={0}, use_global_device_ids=true | all-gather | bytes 1146880 | tf_op jit(solution)/shard_map/all_gather | solution.py:297
  77.9 1.9 %collective-permute-start.4 = (bf16[256,1792]{1,0:T(8,128)(2,1)S(1)}, bf16[256,1792]{1,0:T(8,128)(2,1)}, u32[]{:S(2)}, u32[]{:S(2)}) collective-permute-start(bf16[256,1792]{1,0:T(8,128)(2,1)S(1)} %all_gather.11.s), channel_id=1, source_target_pairs={{0,1},{1,0},{2,3},{3,2},{4,5},{5,4},{6,7},{7,6},{8,9},{9,8},{10,11... | collective-permute-start | bytes 2752520 | tf_op jit(solution)/shard_map/ppermute | solution.py:225
  79.8 0.0 copy-done
  79.8 0.0 copy-done.5
  79.8 0.0 copy-done.6
  79.8 0.0 copy-start.1
  79.8 1.5 %copy-done.1 = bf16[1024,896]{1,0:T(8,128)(2,1)S(1)} copy-done((bf16[1024,896]{1,0:T(8,128)(2,1)S(1)}, bf16[1024,896]{1,0:T(8,128)(2,1)}, u32[]{:S(2)}) %copy-start.1) | copy-done | bytes 1835032
  81.3 2.7 %backward.1 = f32[256,1024]{1,0:T(8,128)S(1)} custom-call(s32[8,7]{1,0:T(8,128)S(1)} %copy-done.5, s32[8,7]{1,0:T(8,128)S(1)} %copy-done.6, bf16[256,1792]{1,0:T(8,128)(2,1)S(1)} %all_gather.11.s, bf16[1024,896]{1,0:T(8,128)(2,1)S(1)} %copy-done, bf16[1024,896]{1,0:T(8,128)(2,1)S(1)} %copy-done.1), custom_call_target="tpu_custom_call" | custom-call | flops 939524096 | bytes 5242880 | tf_op jit(solution)/shard_map/backward/pallas_call | solution.py:191
  84.1 0.0 copy-start.3
  84.1 1.0 copy-done.3
  85.1 0.0 copy-start.2
  85.1 10.0 %all-to-all-start.1 = ((f32[16,16,1024]{2,1,0:T(8,128)}), f32[16,16,1024]{2,1,0:T(8,128)}, u32[]{:S(2)}, u32[]{:S(2)}) async-start(f32[16,16,1024]{2,1,0:T(8,128)} %bitcast.5), calls=%async_computation.1 | async-start | bytes 2097152 | tf_op jit(solution)/shard_map/all_to_all | solution.py:299
  95.0 0.1 pad_add_fusion.place
  95.1 0.0 copy-done.2
  95.1 0.8 turn.1.t
  95.9 0.3 shard_map.93
  96.2 3.5 %collective-permute-start = (bf16[128,1792]{1,0:T(8,128)(2,1)S(1)}, bf16[128,1792]{1,0:T(8,128)(2,1)S(1)}, u32[]{:S(2)}, u32[]{:S(2)}) collective-permute-start(bf16[128,1792]{1,0:T(8,128)(2,1)S(1)} %shard_map.93), channel_id=1, source_target_pairs={{0,64},{1,449},{2,66},{3,451},{4,68},{5,453},{6,70},{7,455},{8,72}... | collective-permute-start | bytes 1376264 | tf_op jit(solution)/shard_map/ppermute | solution.py:232
  99.7 0.0 collective-permute-done.4.s
  99.7 1.7 %shard_map.95 = (bf16[128,1792]{1,0:T(8,128)(2,1)S(1)}, bf16[128,1792]{1,0:T(8,128)(2,1)S(1)}, bf16[128,1792]{1,0:T(8,128)(2,1)S(1)}) custom-call(bf16[5,128,256]{2,1,0:T(8,128)(2,1)S(1)} %turn.1.t, bf16[256,1792]{1,0:T(8,128)(2,1)} %collective-permute-done.4.s), custom_call_target="tpu_custom_call" | custom-call | flops 352321536 | bytes 1376256 | tf_op jit(solution)/shard_map/pallas_call | solution.py:150
  101.4 3.5 %collective-permute-start.5 = (bf16[128,1792]{1,0:T(8,128)(2,1)S(1)}, bf16[128,1792]{1,0:T(8,128)(2,1)S(1)}, u32[]{:S(2)}, u32[]{:S(2)}) collective-permute-start(bf16[128,1792]{1,0:T(8,128)(2,1)S(1)} %get-tuple-element.20), channel_id=1, source_target_pairs={{0,64},{1,449},{2,66},{3,451},{4,68},{5,453},{6,70},{7,455},{8,72}... | collective-permute-start | bytes 1376264 | tf_op jit(solution)/shard_map/ppermute | solution.py:235
  104.9 0.7 shard_map.94
  105.5 2.5 %collective-permute-done.a = bf16[128,1792]{1,0:T(8,128)(2,1)S(1)} collective-permute-done((bf16[128,1792]{1,0:T(8,128)(2,1)S(1)}, bf16[128,1792]{1,0:T(8,128)(2,1)S(1)}, u32[]{:S(2)}, u32[]{:S(2)}) %collective-permute-start) | collective-permute-done | bytes 458784 | tf_op jit(solution)/shard_map/ppermute | solution.py:232
  108.0 0.1 plus.5
  108.1 2.0 %collective-permute-start.1 = (bf16[128,1792]{1,0:T(8,128)(2,1)S(1)}, bf16[128,1792]{1,0:T(8,128)(2,1)S(1)}, u32[]{:S(2)}, u32[]{:S(2)}) collective-permute-start(bf16[128,1792]{1,0:T(8,128)(2,1)S(1)} %plus.5), channel_id=1, source_target_pairs={{0,64},{1,449},{2,66},{3,451},{4,68},{5,453},{6,70},{7,455},{8,72}... | collective-permute-start | bytes 1376264 | tf_op jit(solution)/shard_map/ppermute | solution.py:232
  110.1 2.8 %collective-permute-done.5.a = bf16[128,1792]{1,0:T(8,128)(2,1)S(1)} collective-permute-done((bf16[128,1792]{1,0:T(8,128)(2,1)S(1)}, bf16[128,1792]{1,0:T(8,128)(2,1)S(1)}, u32[]{:S(2)}, u32[]{:S(2)}) %collective-permute-start.5) | collective-permute-done | bytes 458784 | tf_op jit(solution)/shard_map/ppermute | solution.py:235
  113.0 0.1 plus.8
  113.1 2.3 %collective-permute-start.6 = (bf16[128,1792]{1,0:T(8,128)(2,1)S(1)}, bf16[128,1792]{1,0:T(8,128)(2,1)S(1)}, u32[]{:S(2)}, u32[]{:S(2)}) collective-permute-start(bf16[128,1792]{1,0:T(8,128)(2,1)S(1)} %plus.8), channel_id=1, source_target_pairs={{0,64},{1,449},{2,66},{3,451},{4,68},{5,453},{6,70},{7,455},{8,72}... | collective-permute-start | bytes 1376264 | tf_op jit(solution)/shard_map/ppermute | solution.py:235
  115.4 4.3 %collective-permute-done.1.a = bf16[128,1792]{1,0:T(8,128)(2,1)S(1)} collective-permute-done((bf16[128,1792]{1,0:T(8,128)(2,1)S(1)}, bf16[128,1792]{1,0:T(8,128)(2,1)S(1)}, u32[]{:S(2)}, u32[]{:S(2)}) %collective-permute-start.1) | collective-permute-done | bytes 458784 | tf_op jit(solution)/shard_map/ppermute | solution.py:232
  119.7 0.1 plus.6
  119.8 1.9 %collective-permute-start.2 = (bf16[128,1792]{1,0:T(8,128)(2,1)S(1)}, bf16[128,1792]{1,0:T(8,128)(2,1)S(1)}, u32[]{:S(2)}, u32[]{:S(2)}) collective-permute-start(bf16[128,1792]{1,0:T(8,128)(2,1)S(1)} %plus.6), channel_id=1, source_target_pairs={{0,64},{1,449},{2,66},{3,451},{4,68},{5,453},{6,70},{7,455},{8,72}... | collective-permute-start | bytes 1376264 | tf_op jit(solution)/shard_map/ppermute | solution.py:232
  121.7 2.9 %collective-permute-done.6.a = bf16[128,1792]{1,0:T(8,128)(2,1)S(1)} collective-permute-done((bf16[128,1792]{1,0:T(8,128)(2,1)S(1)}, bf16[128,1792]{1,0:T(8,128)(2,1)S(1)}, u32[]{:S(2)}, u32[]{:S(2)}) %collective-permute-start.6) | collective-permute-done | bytes 458784 | tf_op jit(solution)/shard_map/ppermute | solution.py:235
  124.7 0.1 plus.9
  124.8 1.9 %collective-permute-start.7 = (bf16[128,1792]{1,0:T(8,128)(2,1)S(1)}, bf16[128,1792]{1,0:T(8,128)(2,1)S(1)}, u32[]{:S(2)}, u32[]{:S(2)}) collective-permute-start(bf16[128,1792]{1,0:T(8,128)(2,1)S(1)} %plus.9), channel_id=1, source_target_pairs={{0,64},{1,449},{2,66},{3,451},{4,68},{5,453},{6,70},{7,455},{8,72}... | collective-permute-start | bytes 1376264 | tf_op jit(solution)/shard_map/ppermute | solution.py:235
  126.7 4.7 %collective-permute-done.2.a = bf16[128,1792]{1,0:T(8,128)(2,1)S(1)} collective-permute-done((bf16[128,1792]{1,0:T(8,128)(2,1)S(1)}, bf16[128,1792]{1,0:T(8,128)(2,1)S(1)}, u32[]{:S(2)}, u32[]{:S(2)}) %collective-permute-start.2) | collective-permute-done | bytes 458784 | tf_op jit(solution)/shard_map/ppermute | solution.py:232
  131.4 0.1 plus.7
  131.5 1.9 %collective-permute-start.3 = (bf16[128,1792]{1,0:T(8,128)(2,1)S(1)}, bf16[128,1792]{1,0:T(8,128)(2,1)S(1)}, u32[]{:S(2)}, u32[]{:S(2)}) collective-permute-start(bf16[128,1792]{1,0:T(8,128)(2,1)S(1)} %plus.7), channel_id=1, source_target_pairs={{0,64},{1,449},{2,66},{3,451},{4,68},{5,453},{6,70},{7,455},{8,72}... | collective-permute-start | bytes 1376264 | tf_op jit(solution)/shard_map/ppermute | solution.py:232
  133.4 2.9 %collective-permute-done.7 = bf16[128,1792]{1,0:T(8,128)(2,1)S(1)} collective-permute-done((bf16[128,1792]{1,0:T(8,128)(2,1)S(1)}, bf16[128,1792]{1,0:T(8,128)(2,1)S(1)}, u32[]{:S(2)}, u32[]{:S(2)}) %collective-permute-start.7) | collective-permute-done | bytes 458784 | tf_op jit(solution)/shard_map/ppermute | solution.py:235
  136.4 1.9 %collective-permute-start.8 = (bf16[128,1792]{1,0:T(8,128)(2,1)S(1)}, bf16[128,1792]{1,0:T(8,128)(2,1)S(1)}, u32[]{:S(2)}, u32[]{:S(2)}) collective-permute-start(bf16[128,1792]{1,0:T(8,128)(2,1)S(1)} %collective-permute-done.7), channel_id=1, source_target_pairs={{0,1},{1,0},{2,3},{3,2},{4,5},{5,4},{6,7},{7,6},{8,9},{9,8},{10,11... | collective-permute-start | bytes 1376264 | tf_op jit(solution)/shard_map/ppermute | solution.py:238
  138.3 0.0 all-to-all-done.1
  138.3 1.9 %reduce_sum.9 = bf16[16,1024]{1,0:T(8,128)(2,1)} reduce(f32[16,16,1024]{2,1,0:T(8,128)} %all-to-all-done.1, f32[]{:T(128)} %constant.19.clone.1), dimensions={0}, to_apply=%region_0.1 | reduce | flops 245760 | bytes 1081348 | tf_op jit(solution)/shard_map/reduce_sum | solution.py:300
  140.2 2.9 %collective-permute-done.3.refs_0_ = bf16[128,1792]{1,0:T(8,128)(2,1)S(1)} collective-permute-done((bf16[128,1792]{1,0:T(8,128)(2,1)S(1)}, bf16[128,1792]{1,0:T(8,128)(2,1)S(1)}, u32[]{:S(2)}, u32[]{:S(2)}) %collective-permute-start.3) | collective-permute-done | bytes 458784 | tf_op jit(solution)/shard_map/ppermute | solution.py:232
  143.1 0.0 collective-permute-done.8.refs_1_
  143.1 1.6 %finish.1 = (bf16[8,16,896]{2,1,0:T(8,128)(2,1)}, bf16[8,16,896]{2,1,0:T(8,128)(2,1)}) custom-call(s32[8,7]{1,0:T(8,128)S(1)} %copy-done.5, s32[8,7]{1,0:T(8,128)S(1)} %copy-done.6, bf16[128,1792]{1,0:T(8,128)(2,1)S(1)} %collective-permute-done.3.refs_0_, bf16[128,1792]{1,0:T(8,128)(2,1)S(1)} %collective-permute-done.8.refs_1_, ...), custom_call_target="tpu_custom_call" | custom-call | tf_op jit(solution)/shard_map/finish/pallas_call | solution.py:261
Async XLA Ops:
  32.5 25.5 %copy-start.4 = (bf16[64,896]{1,0:T(8,128)(2,1)S(1)}, bf16[64,896]{1,0:T(8,128)(2,1)}, u32[]{:S(2)}) copy-start(bf16[64,896]{1,0:T(8,128)(2,1)} %s.1) | copy-start | bytes 344068
  32.5 47.3 %copy-start = (bf16[1024,896]{1,0:T(8,128)(2,1)S(1)}, bf16[1024,896]{1,0:T(8,128)(2,1)}, u32[]{:S(2)}) copy-start(bf16[1024,896]{1,0:T(8,128)(2,1)} %gw.3) | copy-start | bytes 5505028
  32.5 47.4 %copy-start.5 = (s32[8,7]{1,0:T(8,128)S(1)}, s32[8,7]{1,0:T(8,128)}, u32[]{:S(2)}) copy-start(s32[8,7]{1,0:T(8,128)} %gm.5) | copy-start | bytes 676
  32.5 47.4 %copy-start.6 = (s32[8,7]{1,0:T(8,128)S(1)}, s32[8,7]{1,0:T(8,128)}, u32[]{:S(2)}) copy-start(s32[8,7]{1,0:T(8,128)} %um.5) | copy-start | bytes 676
  77.9 21.8 %collective-permute-start.4 = (bf16[256,1792]{1,0:T(8,128)(2,1)S(1)}, bf16[256,1792]{1,0:T(8,128)(2,1)}, u32[]{:S(2)}, u32[]{:S(2)}) collective-permute-start(bf16[256,1792]{1,0:T(8,128)(2,1)S(1)} %all_gather.11.s), channel_id=1, source_target_pairs={{0,1},{1,0},{2,3},{3,2},{4,5},{5,4},{6,7},{7,6},{8,9},{9,8},{10,11... | collective-permute-start | bytes 2752520 | tf_op jit(solution)/shard_map/ppermute | solution.py:225
  79.8 1.5 %copy-start.1 = (bf16[1024,896]{1,0:T(8,128)(2,1)S(1)}, bf16[1024,896]{1,0:T(8,128)(2,1)}, u32[]{:S(2)}) copy-start(bf16[1024,896]{1,0:T(8,128)(2,1)} %uw.3) | copy-start | bytes 5505028
  84.1 1.0 copy-start.3
  85.1 10.1 %copy-start.2 = (bf16[256,1024]{1,0:T(8,128)(2,1)S(1)}, bf16[256,1024]{1,0:T(8,128)(2,1)}, u32[]{:S(2)}) copy-start(bf16[256,1024]{1,0:T(8,128)(2,1)} %all_gather.10.t) | copy-start | bytes 1572868
  85.1 53.2 %all-to-all-start.1 = ((f32[16,16,1024]{2,1,0:T(8,128)}), f32[16,16,1024]{2,1,0:T(8,128)}, u32[]{:S(2)}, u32[]{:S(2)}) async-start(f32[16,16,1024]{2,1,0:T(8,128)} %bitcast.5), calls=%async_computation.1 | async-start | bytes 2097152 | tf_op jit(solution)/shard_map/all_to_all | solution.py:299
  96.2 11.8 %collective-permute-start = (bf16[128,1792]{1,0:T(8,128)(2,1)S(1)}, bf16[128,1792]{1,0:T(8,128)(2,1)S(1)}, u32[]{:S(2)}, u32[]{:S(2)}) collective-permute-start(bf16[128,1792]{1,0:T(8,128)(2,1)S(1)} %shard_map.93), channel_id=1, source_target_pairs={{0,64},{1,449},{2,66},{3,451},{4,68},{5,453},{6,70},{7,455},{8,72}... | collective-permute-start | bytes 1376264 | tf_op jit(solution)/shard_map/ppermute | solution.py:232
  101.4 11.6 %collective-permute-start.5 = (bf16[128,1792]{1,0:T(8,128)(2,1)S(1)}, bf16[128,1792]{1,0:T(8,128)(2,1)S(1)}, u32[]{:S(2)}, u32[]{:S(2)}) collective-permute-start(bf16[128,1792]{1,0:T(8,128)(2,1)S(1)} %get-tuple-element.20), channel_id=1, source_target_pairs={{0,64},{1,449},{2,66},{3,451},{4,68},{5,453},{6,70},{7,455},{8,72}... | collective-permute-start | bytes 1376264 | tf_op jit(solution)/shard_map/ppermute | solution.py:235
  108.1 11.6 %collective-permute-start.1 = (bf16[128,1792]{1,0:T(8,128)(2,1)S(1)}, bf16[128,1792]{1,0:T(8,128)(2,1)S(1)}, u32[]{:S(2)}, u32[]{:S(2)}) collective-permute-start(bf16[128,1792]{1,0:T(8,128)(2,1)S(1)} %plus.5), channel_id=1, source_target_pairs={{0,64},{1,449},{2,66},{3,451},{4,68},{5,453},{6,70},{7,455},{8,72}... | collective-permute-start | bytes 1376264 | tf_op jit(solution)/shard_map/ppermute | solution.py:232
  113.1 11.6 %collective-permute-start.6 = (bf16[128,1792]{1,0:T(8,128)(2,1)S(1)}, bf16[128,1792]{1,0:T(8,128)(2,1)S(1)}, u32[]{:S(2)}, u32[]{:S(2)}) collective-permute-start(bf16[128,1792]{1,0:T(8,128)(2,1)S(1)} %plus.8), channel_id=1, source_target_pairs={{0,64},{1,449},{2,66},{3,451},{4,68},{5,453},{6,70},{7,455},{8,72}... | collective-permute-start | bytes 1376264 | tf_op jit(solution)/shard_map/ppermute | solution.py:235
  119.8 11.6 %collective-permute-start.2 = (bf16[128,1792]{1,0:T(8,128)(2,1)S(1)}, bf16[128,1792]{1,0:T(8,128)(2,1)S(1)}, u32[]{:S(2)}, u32[]{:S(2)}) collective-permute-start(bf16[128,1792]{1,0:T(8,128)(2,1)S(1)} %plus.6), channel_id=1, source_target_pairs={{0,64},{1,449},{2,66},{3,451},{4,68},{5,453},{6,70},{7,455},{8,72}... | collective-permute-start | bytes 1376264 | tf_op jit(solution)/shard_map/ppermute | solution.py:232
  124.8 11.6 %collective-permute-start.7 = (bf16[128,1792]{1,0:T(8,128)(2,1)S(1)}, bf16[128,1792]{1,0:T(8,128)(2,1)S(1)}, u32[]{:S(2)}, u32[]{:S(2)}) collective-permute-start(bf16[128,1792]{1,0:T(8,128)(2,1)S(1)} %plus.9), channel_id=1, source_target_pairs={{0,64},{1,449},{2,66},{3,451},{4,68},{5,453},{6,70},{7,455},{8,72}... | collective-permute-start | bytes 1376264 | tf_op jit(solution)/shard_map/ppermute | solution.py:235
  131.5 11.6 %collective-permute-start.3 = (bf16[128,1792]{1,0:T(8,128)(2,1)S(1)}, bf16[128,1792]{1,0:T(8,128)(2,1)S(1)}, u32[]{:S(2)}, u32[]{:S(2)}) collective-permute-start(bf16[128,1792]{1,0:T(8,128)(2,1)S(1)} %plus.7), channel_id=1, source_target_pairs={{0,64},{1,449},{2,66},{3,451},{4,68},{5,453},{6,70},{7,455},{8,72}... | collective-permute-start | bytes 1376264 | tf_op jit(solution)/shard_map/ppermute | solution.py:232
  136.4 6.7 %collective-permute-start.8 = (bf16[128,1792]{1,0:T(8,128)(2,1)S(1)}, bf16[128,1792]{1,0:T(8,128)(2,1)S(1)}, u32[]{:S(2)}, u32[]{:S(2)}) collective-permute-start(bf16[128,1792]{1,0:T(8,128)(2,1)S(1)} %collective-permute-done.7), channel_id=1, source_target_pairs={{0,1},{1,0},{2,3},{3,2},{4,5},{5,4},{6,7},{7,6},{8,9},{9,8},{10,11... | collective-permute-start | bytes 1376264 | tf_op jit(solution)/shard_map/ppermute | solution.py:238
where the time goes:
time: 145 us
  blocking collectives  71 us (49%)
  starting transfers between devices  30.8 us (21%)
  waiting for transfers between devices  23.1 us (16%)
  Pallas kernels  14.5 us (10%)
  local copies, waits for them, and re-layouts  2.49 us (2%)
  other arithmetic  1.98 us (1%)
    all_to_all x1, blocking collectives, layer(): received = lax.all_to_all(partial, 'row', 0, 0, tiled=True)  25.5 us
    all_gather x1, blocking collectives, layer(): slopes = lax.all_gather(slopes, 'row', axis=0, tiled=True)  19.1 us
    ppermute x4, waiting for transfers between devices, reduce_parts(): own = lax.ppermute(own, ('dp', 'col'), ring)  14.4 us
    all_gather x1, blocking collectives, gather_tokens(): lax.all_gather(tokens, 'col', axis=0, tiled=True, axis_index_groups=along_x)  13.6 us
    all_gather x1, blocking collectives, gather_tokens(): lax.all_gather(tokens, 'col', axis=0, tiled=True, axis_index_groups=same_x)  12.8 us
    all_to_all x1, starting transfers between devices, layer(): pieces = lax.all_to_all(share, 'col', 0, 0, tiled=True)  9.98 us
    ppermute x4, starting transfers between devices, reduce_parts(): own = lax.ppermute(own, ('dp', 'col'), ring)  9.34 us
    ppermute x3, waiting for transfers between devices, reduce_parts(): other = lax.ppermute(other, ('dp', 'col'), ring)  8.69 us
  transfers between devices with their start and end apart: 10, of which 7 were waited for; matrix products, arithmetic and copies ran while one was open for 1% of the time, Pallas kernels for 5%

commit v1 on v0

--- a/solution.py
+++ b/solution.py
@@ -186,7 +186,7 @@
         prune(live, gw, uw, gm, um, block, pl.program_id(0) * (ROWS // block))
         out[...] = lax.dot_general(
             s[...], live[...], (((1,), (1,)), ((), ())), preferred_element_type=F32
-        )
+        ).astype(BF)
 
     return pl.pallas_call(
         kernel,
@@ -199,7 +199,7 @@
             pl.BlockSpec((ROWS, width), lambda k: (k, 0)),
         ],
         out_specs=pl.BlockSpec((toks, ROWS), lambda k: (0, k)),
-        out_shape=jax.ShapeDtypeStruct((toks, depth), F32),
+        out_shape=jax.ShapeDtypeStruct((toks, depth), BF),
         scratch_shapes=[pltpu.VMEM((ROWS, 2 * width), BF)],
         cost_estimate=pl.CostEstimate(
             flops=4 * toks * depth * width,
@@ -297,7 +297,8 @@
     slopes = lax.all_gather(slopes, "row", axis=0, tiled=True)
     sums, share = reduce_parts(turned, slopes, weights)
     pieces = lax.all_to_all(share, "col", 0, 0, tiled=True)
-    input_grad = jnp.sum(pieces.reshape((cols, -1) + pieces.shape[1:]), axis=0).astype(BF)
+    pieces = pieces.reshape((cols, -1) + pieces.shape[1:])
+    input_grad = jnp.sum(pieces.astype(F32), axis=0).astype(BF)
     gate_grad, up_grad = finish(sums, weights[2], weights[3], block)
     return hidden, input_grad, gate_grad, up_grad
 

time: 145 us -> 143 us (0.986)
  waiting for transfers between devices: 23.1 us -> 15.6 us
  starting transfers between devices: 30.8 us -> 35.6 us
  local copies, waits for them, and re-layouts: 2.49 us -> 0.03 us
  Pallas kernels: 14.5 us -> 16.9 us
    ppermute x3, waiting for transfers between devices: 8.69 us -> 4.85 us  [reduce_parts(): other = lax.ppermute(other, ('dp', 'col'), ring)]
    ppermute x4, waiting for transfers between devices: 14.4 us -> 10.8 us  [reduce_parts(): own = lax.ppermute(own, ('dp', 'col'), ring)]
    ppermute x3, starting transfers between devices: 7.69 us -> 11 us  [reduce_parts(): other = lax.ppermute(other, ('dp', 'col'), ring)]
    pallas_call x5, Pallas kernels: 0.53 us -> 3.16 us  [plus(): pl.pallas_call(kernel, in_specs=[in_vmem(), in_vmem()], out_specs=in_vmem...]
    unnamed x14 -> x12, local copies, waits for them, and re-layouts: 2.49 us -> 0.03 us
    all_to_all x1, starting transfers between devices: 9.98 us -> 11.5 us  [layer(): pieces = lax.all_to_all(share, 'col', 0, 0, tiled=True)]
  transfers between devices with their start and end apart: 10 -> 10, of which waited for: 7 -> 5; matrix products, arithmetic and copies ran while one was open for 1% -> 1% of each run, Pallas kernels for 5% -> 6%
where the time goes in v1:
time: 143 us; the launch traced here: 142 us
  blocking collectives  71 us (50%)
  starting transfers between devices  35.6 us (25%)
  Pallas kernels  16.9 us (12%)
  waiting for transfers between devices  15.6 us (11%)
  other arithmetic  1.82 us (1%)
    all_to_all x1, blocking collectives, layer(): received = lax.all_to_all(partial, 'row', 0, 0, tiled=True)  25.5 us
    all_gather x1, blocking collectives, layer(): slopes = lax.all_gather(slopes, 'row', axis=0, tiled=True)  19.1 us
    all_gather x1, blocking collectives, gather_tokens(): lax.all_gather(tokens, 'col', axis=0, tiled=True, axis_index_groups=along_x)  13.6 us
    all_gather x1, blocking collectives, gather_tokens(): lax.all_gather(tokens, 'col', axis=0, tiled=True, axis_index_groups=same_x)  12.8 us
    all_to_all x1, starting transfers between devices, layer(): pieces = lax.all_to_all(share, 'col', 0, 0, tiled=True)  11.5 us
    ppermute x3, starting transfers between devices, reduce_parts(): other = lax.ppermute(other, ('dp', 'col'), ring)  11 us
    ppermute x4, waiting for transfers between devices, reduce_parts(): own = lax.ppermute(own, ('dp', 'col'), ring)  10.8 us
    ppermute x4, starting transfers between devices, reduce_parts(): own = lax.ppermute(own, ('dp', 'col'), ring)  9.34 us
  transfers between devices with their start and end apart: 10, of which 5 were waited for; matrix products, arithmetic and copies ran while one was open for 1% of the time, Pallas kernels for 6%

profile of v1, /device:TPU:6, one launch (start us, length us, event | category | flops | bytes accessed | tf_op | source)
XLA Modules:
  0.0 141.8 jit_solution(8722265776483339800)
XLA Ops:
  0.6 12.8 %all_gather.9 = bf16[64,1024]{1,0:T(8,128)(2,1)S(1)} all-gather(bf16[16,1024]{1,0:T(8,128)(2,1)} %param.6), channel_id=1, replica_groups={{0,1,2,3},{4,5,6,7},{8,9,10,11},{12,13,14,15},{16,17,18,19},{20,21,22,2..., dimensions={0}, use_global_device_ids=true | all-gather | bytes 163840 | tf_op jit(solution)/shard_map/all_gather | solution.py:276
  13.5 13.6 %all_gather.10.t = bf16[256,1024]{1,0:T(8,128)(2,1)} all-gather(bf16[64,1024]{1,0:T(8,128)(2,1)S(1)} %all_gather.9), channel_id=1, replica_groups={{0,4,8,12},{1,5,9,13},{2,6,10,14},{3,7,11,15},{16,20,24,28},{17,21,25,2..., dimensions={0}, use_global_device_ids=true | all-gather | bytes 655360 | tf_op jit(solution)/shard_map/all_gather | solution.py:277
  27.0 5.4 %forward.1 = bf16[256,1792]{1,0:T(8,128)(2,1)} custom-call(s32[8,7]{1,0:T(8,128)} %gm.5, s32[8,7]{1,0:T(8,128)} %um.5, bf16[256,1024]{1,0:T(8,128)(2,1)} %all_gather.10.t, bf16[1024,896]{1,0:T(8,128)(2,1)} %gw.3, bf16[1024,896]{1,0:T(8,128)(2,1)} %uw.3), custom_call_target="tpu_custom_call" | custom-call | flops 939524096 | bytes 5242880 | tf_op jit(solution)/shard_map/forward/pallas_call | solution.py:55
  32.5 0.0 copy-start.3
  32.5 0.0 copy-start.2
  32.5 25.5 %all_to_all.20 = bf16[4,64,1792]{2,1,0:T(8,128)(2,1)S(1)} all-to-all(bf16[4,64,1792]{2,1,0:T(8,128)(2,1)} %bitcast.6), channel_id=1, replica_groups=mesh['dp'=8,'row'=4,'col'=16] {'row'}, dimensions={0} | all-to-all | bytes 1835008 | tf_op jit(solution)/shard_map/all_to_all | solution.py:294
  57.9 0.0 copy-done.3
  57.9 0.8 activate.1
  58.7 19.1 %all_gather.11.s = bf16[256,1792]{1,0:T(8,128)(2,1)S(1)} all-gather(bf16[64,1792]{1,0:T(8,128)(2,1)S(1)} %get-tuple-element.16), channel_id=1, replica_groups=mesh['dp'=8,'row'=4,'col'=16] {'row'}, dimensions={0}, use_global_device_ids=true | all-gather | bytes 1146880 | tf_op jit(solution)/shard_map/all_gather | solution.py:297
  77.8 1.9 %collective-permute-start.4 = (bf16[256,1792]{1,0:T(8,128)(2,1)S(1)}, bf16[256,1792]{1,0:T(8,128)(2,1)S(1)}, u32[]{:S(2)}, u32[]{:S(2)}) collective-permute-start(bf16[256,1792]{1,0:T(8,128)(2,1)S(1)} %all_gather.11.s), channel_id=1, source_target_pairs={{0,1},{1,0},{2,3},{3,2},{4,5},{5,4},{6,7},{7,6},{8,9},{9,8},{10,11... | collective-permute-start | bytes 2752520 | tf_op jit(solution)/shard_map/ppermute | solution.py:225
  79.8 0.1 pad_add_fusion.place
  79.9 0.0 copy-done.2
  79.9 0.8 turn.1.t
  80.6 0.3 shard_map.93
  80.9 3.5 %collective-permute-start = (bf16[128,1792]{1,0:T(8,128)(2,1)S(1)}, bf16[128,1792]{1,0:T(8,128)(2,1)S(1)}, u32[]{:S(2)}, u32[]{:S(2)}) collective-permute-start(bf16[128,1792]{1,0:T(8,128)(2,1)S(1)} %shard_map.93), channel_id=1, source_target_pairs={{0,64},{1,449},{2,66},{3,451},{4,68},{5,453},{6,70},{7,455},{8,72}... | collective-permute-start | bytes 1376264 | tf_op jit(solution)/shard_map/ppermute | solution.py:232
  84.4 0.0 collective-permute-done.4.s
  84.4 0.5 shard_map.95
  85.0 0.0 copy-start
  85.0 0.0 copy-start.1
  85.0 0.0 copy-start.4
  85.0 0.0 copy-start.5
  85.0 3.7 %collective-permute-start.5 = (bf16[128,1792]{1,0:T(8,128)(2,1)S(1)}, bf16[128,1792]{1,0:T(8,128)(2,1)S(1)}, u32[]{:S(2)}, u32[]{:S(2)}) collective-permute-start(bf16[128,1792]{1,0:T(8,128)(2,1)S(1)} %get-tuple-element.20), channel_id=1, source_target_pairs={{0,64},{1,449},{2,66},{3,451},{4,68},{5,453},{6,70},{7,455},{8,72}... | collective-permute-start | bytes 1376264 | tf_op jit(solution)/shard_map/ppermute | solution.py:235
  88.8 0.7 shard_map.94
  89.4 3.3 %collective-permute-done.a = bf16[128,1792]{1,0:T(8,128)(2,1)S(1)} collective-permute-done((bf16[128,1792]{1,0:T(8,128)(2,1)S(1)}, bf16[128,1792]{1,0:T(8,128)(2,1)S(1)}, u32[]{:S(2)}, u32[]{:S(2)}) %collective-permute-start) | collective-permute-done | bytes 458784 | tf_op jit(solution)/shard_map/ppermute | solution.py:232
  92.7 0.9 plus.5
  93.7 2.0 %collective-permute-start.1 = (bf16[128,1792]{1,0:T(8,128)(2,1)}, bf16[128,1792]{1,0:T(8,128)(2,1)}, u32[]{:S(2)}, u32[]{:S(2)}) collective-permute-start(bf16[128,1792]{1,0:T(8,128)(2,1)} %plus.5), channel_id=1, source_target_pairs={{0,64},{1,449},{2,66},{3,451},{4,68},{5,453},{6,70},{7,455},{8,72}... | collective-permute-start | bytes 1376264 | tf_op jit(solution)/shard_map/ppermute | solution.py:232
  95.7 2.0 %collective-permute-done.5.a = bf16[128,1792]{1,0:T(8,128)(2,1)S(1)} collective-permute-done((bf16[128,1792]{1,0:T(8,128)(2,1)S(1)}, bf16[128,1792]{1,0:T(8,128)(2,1)S(1)}, u32[]{:S(2)}, u32[]{:S(2)}) %collective-permute-start.5) | collective-permute-done | bytes 458784 | tf_op jit(solution)/shard_map/ppermute | solution.py:235
  97.7 0.9 plus.8
  98.5 2.0 %collective-permute-start.6 = (bf16[128,1792]{1,0:T(8,128)(2,1)}, bf16[128,1792]{1,0:T(8,128)(2,1)S(1)}, u32[]{:S(2)}, u32[]{:S(2)}) collective-permute-start(bf16[128,1792]{1,0:T(8,128)(2,1)} %plus.8), channel_id=1, source_target_pairs={{0,64},{1,449},{2,66},{3,451},{4,68},{5,453},{6,70},{7,455},{8,72}... | collective-permute-start | bytes 1376264 | tf_op jit(solution)/shard_map/ppermute | solution.py:235
  100.6 0.0 copy-done
  100.6 0.0 copy-done.1
  100.6 0.0 copy-done.4
  100.6 0.0 copy-done.5
  100.6 3.6 %backward.1 = bf16[256,1024]{1,0:T(8,128)(2,1)} custom-call(s32[8,7]{1,0:T(8,128)S(1)} %copy-done.4, s32[8,7]{1,0:T(8,128)S(1)} %copy-done.5, bf16[256,1792]{1,0:T(8,128)(2,1)S(1)} %all_gather.11.s, bf16[1024,896]{1,0:T(8,128)(2,1)S(1)} %copy-done, bf16[1024,896]{1,0:T(8,128)(2,1)S(1)} %copy-done.1), custom_call_target="tpu_custom_call" | custom-call | flops 939524096 | bytes 5242880 | tf_op jit(solution)/shard_map/backward/pallas_call | solution.py:191
  104.2 11.5 %all-to-all-start.1 = ((bf16[16,16,1024]{2,1,0:T(8,128)(2,1)}), bf16[16,16,1024]{2,1,0:T(8,128)(2,1)}, u32[]{:S(2)}, u32[]{:S(2)}) async-start(bf16[16,16,1024]{2,1,0:T(8,128)(2,1)} %bitcast.2), calls=%async_computation.1 | async-start | bytes 1048576 | tf_op jit(solution)/shard_map/all_to_all | solution.py:299
  115.8 0.0 collective-permute-done.1.a
  115.8 1.1 plus.6
  116.9 1.9 %collective-permute-start.2 = (bf16[128,1792]{1,0:T(8,128)(2,1)S(1)}, bf16[128,1792]{1,0:T(8,128)(2,1)S(1)}, u32[]{:S(2)}, u32[]{:S(2)}) collective-permute-start(bf16[128,1792]{1,0:T(8,128)(2,1)S(1)} %plus.6), channel_id=1, source_target_pairs={{0,64},{1,449},{2,66},{3,451},{4,68},{5,453},{6,70},{7,455},{8,72}... | collective-permute-start | bytes 1376264 | tf_op jit(solution)/shard_map/ppermute | solution.py:232
  118.8 0.0 collective-permute-done.6.a
  118.8 0.1 plus.9
  118.9 5.2 %collective-permute-start.7 = (bf16[128,1792]{1,0:T(8,128)(2,1)S(1)}, bf16[128,1792]{1,0:T(8,128)(2,1)S(1)}, u32[]{:S(2)}, u32[]{:S(2)}) collective-permute-start(bf16[128,1792]{1,0:T(8,128)(2,1)S(1)} %plus.9), channel_id=1, source_target_pairs={{0,64},{1,449},{2,66},{3,451},{4,68},{5,453},{6,70},{7,455},{8,72}... | collective-permute-start | bytes 1376264 | tf_op jit(solution)/shard_map/ppermute | solution.py:235
  124.1 4.3 %collective-permute-done.2.a = bf16[128,1792]{1,0:T(8,128)(2,1)S(1)} collective-permute-done((bf16[128,1792]{1,0:T(8,128)(2,1)S(1)}, bf16[128,1792]{1,0:T(8,128)(2,1)S(1)}, u32[]{:S(2)}, u32[]{:S(2)}) %collective-permute-start.2) | collective-permute-done | bytes 458784 | tf_op jit(solution)/shard_map/ppermute | solution.py:232
  128.5 0.1 plus.7
  128.6 1.9 %collective-permute-start.3 = (bf16[128,1792]{1,0:T(8,128)(2,1)S(1)}, bf16[128,1792]{1,0:T(8,128)(2,1)S(1)}, u32[]{:S(2)}, u32[]{:S(2)}) collective-permute-start(bf16[128,1792]{1,0:T(8,128)(2,1)S(1)} %plus.7), channel_id=1, source_target_pairs={{0,64},{1,449},{2,66},{3,451},{4,68},{5,453},{6,70},{7,455},{8,72}... | collective-permute-start | bytes 1376264 | tf_op jit(solution)/shard_map/ppermute | solution.py:232
  130.5 2.9 %collective-permute-done.7 = bf16[128,1792]{1,0:T(8,128)(2,1)S(1)} collective-permute-done((bf16[128,1792]{1,0:T(8,128)(2,1)S(1)}, bf16[128,1792]{1,0:T(8,128)(2,1)S(1)}, u32[]{:S(2)}, u32[]{:S(2)}) %collective-permute-start.7) | collective-permute-done | bytes 458784 | tf_op jit(solution)/shard_map/ppermute | solution.py:235
  133.4 1.9 %collective-permute-start.8 = (bf16[128,1792]{1,0:T(8,128)(2,1)S(1)}, bf16[128,1792]{1,0:T(8,128)(2,1)S(1)}, u32[]{:S(2)}, u32[]{:S(2)}) collective-permute-start(bf16[128,1792]{1,0:T(8,128)(2,1)S(1)} %collective-permute-done.7), channel_id=1, source_target_pairs={{0,1},{1,0},{2,3},{3,2},{4,5},{5,4},{6,7},{7,6},{8,9},{9,8},{10,11... | collective-permute-start | bytes 1376264 | tf_op jit(solution)/shard_map/ppermute | solution.py:238
  135.3 0.0 all-to-all-done.1
  135.3 1.7 %reduce_sum.12 = bf16[16,1024]{1,0:T(8,128)(2,1)} reduce(bf16[16,16,1024]{2,1,0:T(8,128)(2,1)} %all-to-all-done.1, bf16[]{:T(256)} %constant.20.clone.1), dimensions={0}, to_apply=%region_0.1 | reduce | flops 245760 | bytes 557058 | tf_op jit(solution)/shard_map/reduce_sum | solution.py:301
  137.1 3.1 %collective-permute-done.3.refs_0_ = bf16[128,1792]{1,0:T(8,128)(2,1)S(1)} collective-permute-done((bf16[128,1792]{1,0:T(8,128)(2,1)S(1)}, bf16[128,1792]{1,0:T(8,128)(2,1)S(1)}, u32[]{:S(2)}, u32[]{:S(2)}) %collective-permute-start.3) | collective-permute-done | bytes 458784 | tf_op jit(solution)/shard_map/ppermute | solution.py:232
  140.2 0.0 collective-permute-done.8.refs_1_
  140.2 1.6 %finish.1 = (bf16[8,16,896]{2,1,0:T(8,128)(2,1)}, bf16[8,16,896]{2,1,0:T(8,128)(2,1)}) custom-call(s32[8,7]{1,0:T(8,128)S(1)} %copy-done.4, s32[8,7]{1,0:T(8,128)S(1)} %copy-done.5, bf16[128,1792]{1,0:T(8,128)(2,1)S(1)} %collective-permute-done.3.refs_0_, bf16[128,1792]{1,0:T(8,128)(2,1)S(1)} %collective-permute-done.8.refs_1_, ...), custom_call_target="tpu_custom_call" | custom-call | tf_op jit(solution)/shard_map/finish/pallas_call | solution.py:261
Async XLA Ops:
  32.5 25.5 %copy-start.3 = (bf16[64,896]{1,0:T(8,128)(2,1)S(1)}, bf16[64,896]{1,0:T(8,128)(2,1)}, u32[]{:S(2)}) copy-start(bf16[64,896]{1,0:T(8,128)(2,1)} %s.1) | copy-start | bytes 344068
  32.5 47.4 %copy-start.2 = (bf16[256,1024]{1,0:T(8,128)(2,1)S(1)}, bf16[256,1024]{1,0:T(8,128)(2,1)}, u32[]{:S(2)}) copy-start(bf16[256,1024]{1,0:T(8,128)(2,1)} %all_gather.10.t) | copy-start | bytes 1572868
  77.8 6.6 %collective-permute-start.4 = (bf16[256,1792]{1,0:T(8,128)(2,1)S(1)}, bf16[256,1792]{1,0:T(8,128)(2,1)S(1)}, u32[]{:S(2)}, u32[]{:S(2)}) collective-permute-start(bf16[256,1792]{1,0:T(8,128)(2,1)S(1)} %all_gather.11.s), channel_id=1, source_target_pairs={{0,1},{1,0},{2,3},{3,2},{4,5},{5,4},{6,7},{7,6},{8,9},{9,8},{10,11... | collective-permute-start | bytes 2752520 | tf_op jit(solution)/shard_map/ppermute | solution.py:225
  80.9 11.8 %collective-permute-start = (bf16[128,1792]{1,0:T(8,128)(2,1)S(1)}, bf16[128,1792]{1,0:T(8,128)(2,1)S(1)}, u32[]{:S(2)}, u32[]{:S(2)}) collective-permute-start(bf16[128,1792]{1,0:T(8,128)(2,1)S(1)} %shard_map.93), channel_id=1, source_target_pairs={{0,64},{1,449},{2,66},{3,451},{4,68},{5,453},{6,70},{7,455},{8,72}... | collective-permute-start | bytes 1376264 | tf_op jit(solution)/shard_map/ppermute | solution.py:232
  85.0 15.6 %copy-start = (bf16[1024,896]{1,0:T(8,128)(2,1)S(1)}, bf16[1024,896]{1,0:T(8,128)(2,1)}, u32[]{:S(2)}) copy-start(bf16[1024,896]{1,0:T(8,128)(2,1)} %gw.3) | copy-start | bytes 5505028
  85.0 15.6 %copy-start.1 = (bf16[1024,896]{1,0:T(8,128)(2,1)S(1)}, bf16[1024,896]{1,0:T(8,128)(2,1)}, u32[]{:S(2)}) copy-start(bf16[1024,896]{1,0:T(8,128)(2,1)} %uw.3) | copy-start | bytes 5505028
  85.0 15.6 %copy-start.4 = (s32[8,7]{1,0:T(8,128)S(1)}, s32[8,7]{1,0:T(8,128)}, u32[]{:S(2)}) copy-start(s32[8,7]{1,0:T(8,128)} %gm.5) | copy-start | bytes 676
  85.0 15.6 %copy-start.5 = (s32[8,7]{1,0:T(8,128)S(1)}, s32[8,7]{1,0:T(8,128)}, u32[]{:S(2)}) copy-start(s32[8,7]{1,0:T(8,128)} %um.5) | copy-start | bytes 676
  85.0 12.7 %collective-permute-start.5 = (bf16[128,1792]{1,0:T(8,128)(2,1)S(1)}, bf16[128,1792]{1,0:T(8,128)(2,1)S(1)}, u32[]{:S(2)}, u32[]{:S(2)}) collective-permute-start(bf16[128,1792]{1,0:T(8,128)(2,1)S(1)} %get-tuple-element.20), channel_id=1, source_target_pairs={{0,64},{1,449},{2,66},{3,451},{4,68},{5,453},{6,70},{7,455},{8,72}... | collective-permute-start | bytes 1376264 | tf_op jit(solution)/shard_map/ppermute | solution.py:235
  93.7 22.1 %collective-permute-start.1 = (bf16[128,1792]{1,0:T(8,128)(2,1)}, bf16[128,1792]{1,0:T(8,128)(2,1)}, u32[]{:S(2)}, u32[]{:S(2)}) collective-permute-start(bf16[128,1792]{1,0:T(8,128)(2,1)} %plus.5), channel_id=1, source_target_pairs={{0,64},{1,449},{2,66},{3,451},{4,68},{5,453},{6,70},{7,455},{8,72}... | collective-permute-start | bytes 1376264 | tf_op jit(solution)/shard_map/ppermute | solution.py:232
  98.5 20.3 %collective-permute-start.6 = (bf16[128,1792]{1,0:T(8,128)(2,1)}, bf16[128,1792]{1,0:T(8,128)(2,1)S(1)}, u32[]{:S(2)}, u32[]{:S(2)}) collective-permute-start(bf16[128,1792]{1,0:T(8,128)(2,1)} %plus.8), channel_id=1, source_target_pairs={{0,64},{1,449},{2,66},{3,451},{4,68},{5,453},{6,70},{7,455},{8,72}... | collective-permute-start | bytes 1376264 | tf_op jit(solution)/shard_map/ppermute | solution.py:235
  104.2 31.1 %all-to-all-start.1 = ((bf16[16,16,1024]{2,1,0:T(8,128)(2,1)}), bf16[16,16,1024]{2,1,0:T(8,128)(2,1)}, u32[]{:S(2)}, u32[]{:S(2)}) async-start(bf16[16,16,1024]{2,1,0:T(8,128)(2,1)} %bitcast.2), calls=%async_computation.1 | async-start | bytes 1048576 | tf_op jit(solution)/shard_map/all_to_all | solution.py:299
  116.9 11.6 %collective-permute-start.2 = (bf16[128,1792]{1,0:T(8,128)(2,1)S(1)}, bf16[128,1792]{1,0:T(8,128)(2,1)S(1)}, u32[]{:S(2)}, u32[]{:S(2)}) collective-permute-start(bf16[128,1792]{1,0:T(8,128)(2,1)S(1)} %plus.6), channel_id=1, source_target_pairs={{0,64},{1,449},{2,66},{3,451},{4,68},{5,453},{6,70},{7,455},{8,72}... | collective-permute-start | bytes 1376264 | tf_op jit(solution)/shard_map/ppermute | solution.py:232
  118.9 14.4 %collective-permute-start.7 = (bf16[128,1792]{1,0:T(8,128)(2,1)S(1)}, bf16[128,1792]{1,0:T(8,128)(2,1)S(1)}, u32[]{:S(2)}, u32[]{:S(2)}) collective-permute-start(bf16[128,1792]{1,0:T(8,128)(2,1)S(1)} %plus.9), channel_id=1, source_target_pairs={{0,64},{1,449},{2,66},{3,451},{4,68},{5,453},{6,70},{7,455},{8,72}... | collective-permute-start | bytes 1376264 | tf_op jit(solution)/shard_map/ppermute | solution.py:235
  128.6 11.6 %collective-permute-start.3 = (bf16[128,1792]{1,0:T(8,128)(2,1)S(1)}, bf16[128,1792]{1,0:T(8,128)(2,1)S(1)}, u32[]{:S(2)}, u32[]{:S(2)}) collective-permute-start(bf16[128,1792]{1,0:T(8,128)(2,1)S(1)} %plus.7), channel_id=1, source_target_pairs={{0,64},{1,449},{2,66},{3,451},{4,68},{5,453},{6,70},{7,455},{8,72}... | collective-permute-start | bytes 1376264 | tf_op jit(solution)/shard_map/ppermute | solution.py:232
  133.4 6.8 %collective-permute-start.8 = (bf16[128,1792]{1,0:T(8,128)(2,1)S(1)}, bf16[128,1792]{1,0:T(8,128)(2,1)S(1)}, u32[]{:S(2)}, u32[]{:S(2)}) collective-permute-start(bf16[128,1792]{1,0:T(8,128)(2,1)S(1)} %collective-permute-done.7), channel_id=1, source_target_pairs={{0,1},{1,0},{2,3},{3,2},{4,5},{5,4},{6,7},{7,6},{8,9},{9,8},{10,11... | collective-permute-start | bytes 1376264 | tf_op jit(solution)/shard_map/ppermute | solution.py:238
